TPU v7x, 32 devices: a whole 2x2x4 slice. The times are simulated.
32 devices in a mesh: vec: 4 (over y, x), orb: 8 (over z, core).
Axes of the slice: x: 2, y: 2, z: 4, core: 2. Of those that a mesh axis runs over, the one named last changes fastest.
Arguments:
- chol_occ: float32 [44, 96, 1056], P('vec', 'orb'), may hold values from -6 to 6
- chol_vir: float32 [44, 960, 1056], P('vec', 'orb'), may hold values from -6 to 6
- singles: float32 [96, 960], P('orb'), may hold values from -0.6 to 0.6
Outputs:
- dressed_vir: float32 [44, 960, 1056], P('vec', 'orb')
- dressed_ov: float32 [44, 96, 960], P(None, 'orb', 'vec')
- fock_ov: float32 [96, 960], P('orb')
All inputs are finite; a program needn't handle non-finite values.
Results may differ from a plain program's by a relative error of at most 0.000086.
Values sent between devices are 32-bit elements; how exact they have to be, the bound alone decides.
A program may use at most 64 MiB of HBM per device.

v0:
```python
import jax
import jax.numpy as jnp
from jax import lax
from jax.sharding import PartitionSpec as P


def dress_right(matrix_rows, amplitudes):
    occ_width = amplitudes.shape[0]
    occ_cols = matrix_rows[:, :, :occ_width]
    extra_term = jnp.einsum("qrj,ja->qra", occ_cols, amplitudes, precision=lax.Precision.HIGHEST)
    return jnp.concatenate([occ_cols, matrix_rows[:, :, occ_width:] + extra_term], axis=2)


def dress_left(vir_rows, occ_all, amp_cols):
    return vir_rows - jnp.einsum("qin,ia->qan", occ_all, amp_cols, precision=lax.Precision.HIGHEST)


def shards(chol_occ, chol_vir, singles):
    amplitudes = lax.all_gather(singles, "orb", axis=0, tiled=True)
    occ_width = amplitudes.shape[0]
    vir_local = chol_vir.shape[1]
    vir_start = lax.axis_index("orb") * vir_local
    amp_cols = lax.dynamic_slice_in_dim(amplitudes, vir_start, vir_local, 1)
    occ_all = lax.all_gather(chol_occ, "orb", axis=1, tiled=True)
    dressed_vir = dress_right(dress_left(chol_vir, occ_all, amp_cols), amplitudes)
    dressed_occ = dress_right(chol_occ, amplitudes)
    local_rows = chol_occ.shape[1]
    first_row = lax.axis_index("orb") * local_rows
    row_ids = lax.broadcasted_iota(jnp.int32, (local_rows, chol_occ.shape[2]), 0) + first_row
    col_ids = lax.broadcasted_iota(jnp.int32, (local_rows, chol_occ.shape[2]), 1)
    diag_mask = jnp.where(row_ids == col_ids, 1.0, 0.0).astype(jnp.float32)
    traces_local = jnp.sum(chol_occ * diag_mask[None], axis=(1, 2))
    traces = lax.psum(traces_local, "orb")
    ov_block = dressed_occ[:, :, occ_width:]
    total_vectors = chol_occ.shape[0] * lax.axis_size("vec")
    fock_part = (
        jnp.einsum("q,qia->ia", traces, ov_block, precision=lax.Precision.HIGHEST) / total_vectors
    )
    fock_ov = lax.psum(fock_part, "vec")
    pair_blocks = lax.all_to_all(ov_block, "vec", split_axis=2, concat_axis=0, tiled=True)
    return (dressed_vir, pair_blocks, fock_ov)


def solution(mesh):
    return jax.shard_map(
        shards,
        mesh=mesh,
        in_specs=(P("vec", "orb", None), P("vec", "orb", None), P("orb", None)),
        out_specs=(P("vec", "orb", None), P(None, "orb", "vec"), P("orb", None)),
        check_vma=False,
    )
```

profile of v0, /device:TPU:0, one launch (start us, length us, event | category | flops | bytes accessed | tf_op | source)
XLA Modules:
  0.0 127.6 jit_solution(5254257879419233849)
XLA Ops:
  7.2 0.0 all-gather.3.cloned.1.call-start
  7.2 2.3 %copy.10 = f32[11,12,1056]{2,0,1:T(8,128)} copy(f32[11,12,1056]{2,1,0:T(8,128)} %param.3) | data formatting | bytes 1115136 | tf_op args[0]
  9.5 0.0 all-gather.3.cloned.1.call-update
  9.5 16.7 %all-gather = f32[8,12,960]{2,1,0:T(8,128)S(1)} all-gather(f32[1,12,960]{2,1,0:T(8,128)} %bitcast.22), channel_id=1, replica_groups=mesh['vec'=4,'orb'=8] {'orb'}, dimensions={0}, use_global_device_ids=true | all-gather | bytes 414720 | tf_op jit(solution)/shard_map/all_gather | solution.py:19
  26.3 1.9 %convolution_add_fusion = f32[11,12,960]{2,1,0:T(8,128)S(1)} fusion(f32[96,960,1]{1,0,2:T(8,128)S(1)} %reshape.23, f32[11,12,1056]{2,1,0:T(8,128)} %param.3), kind=kOutput, calls=%fused_computation.4 | convolution fusion | flops 146108160 | bytes 1433088 | tf_op jit(solution)/shard_map/qrj,ja->qra/dot_general | solution.py:10
  28.2 6.0 %copy.13 = f32[11,12,960]{1,0,2:T(8,128)} copy(f32[11,12,960]{2,1,0:T(8,128)S(1)} %convolution_add_fusion) | data formatting | bytes 1013760 | tf_op jit(solution)/shard_map/add | solution.py:11
  34.2 0.0 copy-start
  34.2 6.5 %reshape.27 = f32[4,1,31680]{2,1,0:T(1,128)} reshape(f32[960,11,12]{2,1,0:T(8,128)} %bitcast.20) | data formatting | bytes 1013760
  40.7 0.1 fusion.4
  40.8 0.0 copy-done
  40.8 0.2 multiply_reduce_fusion
  41.0 3.7 %all-to-all-start = ((f32[4,1,31680]{2,1,0:T(1,128)}), f32[4,1,31680]{2,1,0:T(1,128)S(1)}, u32[]{:S(2)}, u32[]{:S(2)}) async-start(f32[4,1,31680]{2,1,0:T(1,128)} %reshape.27), calls=%async_computation | async-start | bytes 1015808 | tf_op jit(solution)/shard_map/all_to_all | solution.py:40
  44.7 19.3 %psum.14 = f32[11]{0:T(128)S(1)} all-reduce(f32[11]{0:T(128)S(1)} %multiply_reduce_fusion), channel_id=1, replica_groups=mesh['vec'=4,'orb'=8] {'orb'}, use_global_device_ids=true, to_apply=%region_1.2 | all-reduce | flops 11 | bytes 88 | tf_op jit(solution)/shard_map/psum | solution.py:33
  64.0 0.8 fusion.1
  64.9 17.7 %psum.15 = f32[12,960]{1,0:T(8,128)} all-reduce(f32[12,960]{1,0:T(8,128)S(1)} %bitcast_multiply_fusion), channel_id=1, replica_groups=mesh['vec'=4,'orb'=8] {'vec'}, use_global_device_ids=true, to_apply=%region_2.3 | all-reduce | flops 11520 | bytes 92160 | tf_op jit(solution)/shard_map/psum | solution.py:39
  82.5 0.0 all-to-all-done
  82.5 0.5 broadcast.18
  83.0 2.1 %reduce = f32[4,31680]{1,0:T(4,128)S(1)} reduce(f32[4,1,31680]{2,1,0:T(1,128)S(1)} %all-to-all-done, f32[]{:T(128)} %broadcast.18), dimensions={1}, to_apply=%all_to_all.13.reduce_sub_computation | reduce | bytes 1013764 | tf_op jit(solution)/shard_map/all_to_all | solution.py:40
  85.2 6.0 %reshape.28 = f32[960,11,12]{2,1,0:T(8,128)} reshape(f32[4,31680]{1,0:T(4,128)S(1)} %reduce) | data formatting | bytes 1013760
  91.2 6.2 %copy.14 = f32[11,12,4,240]{3,0,2,1:T(8,128)S(1)} copy(f32[11,12,4,240]{1,0,3,2:T(8,128)} %bitcast.19) | data formatting | bytes 1013760 | tf_op jit(solution)/shard_map/all_to_all | solution.py:40
  97.4 0.9 all_to_all.16
  98.3 0.0 all-gather.3.cloned.1.call-done
  98.3 14.5 %bitcast_subtract_fusion = f32[11,120,1056]{1,2,0:T(8,128)S(1)} fusion(f32[11,120,1056]{1,2,0:T(8,128)} %param.4, f32[11,96,1056]{2,0,1:T(8,128)} %all-gather.3.cloned.1.call-done, f32[96,960]{1,0:T(8,128)S(1)} %reshape.21, s32[]{:T(128)S(6)} %select_n.11), kind=kOutput, calls=%fused_computation.1 | convolution fusion | flops 1607189760 | bytes 15661060 | tf_op jit(solution)/shard_map/qin,ia->qan/dot_general | solution.py:15
  112.9 4.7 %slice_add_fusion = f32[11,120,960]{1,2,0:T(8,128)S(1)} fusion(f32[11,120,1056]{1,2,0:T(8,128)S(1)} %bitcast_subtract_fusion, f32[96,960,1]{1,0,2:T(8,128)S(1)} %reshape.23), kind=kOutput, calls=%fused_computation.2 | convolution fusion | flops 1461081600 | bytes 11013120 | tf_op jit(solution)/shard_map/qrj,ja->qra/dot_general | solution.py:10
  117.6 3.2 %pad_maximum_fusion = f32[11,120,1056]{1,2,0:T(8,128)} fusion(f32[11,120,960]{1,2,0:T(8,128)S(1)} %slice_add_fusion, f32[11,120,96]{1,2,0:T(8,128)S(1)} %slice.16), kind=kLoop, calls=%fused_computation | loop fusion | flops 1393920 | bytes 11151360 | tf_op jit(solution)/shard_map/concatenate | solution.py:11
  (5 shorter events, 0.1 us)
Async XLA Ops:
  7.2 91.1 %all-gather.3.cloned.1.call-start = ((), (), s32[]{:S(2)}) async-start(), calls=%async_computation.1 | async-start | bytes 7962624 | tf_op jit(solution)/shard_map/all_gather | solution.py:24
  34.2 6.6 %copy-start = (f32[11,12,1056]{2,1,0:T(8,128)S(1)}, f32[11,12,1056]{2,1,0:T(8,128)}, u32[]{:S(2)}) copy-start(f32[11,12,1056]{2,1,0:T(8,128)} %param.3) | copy-start | bytes 1672708
  41.0 41.6 %all-to-all-start = ((f32[4,1,31680]{2,1,0:T(1,128)}), f32[4,1,31680]{2,1,0:T(1,128)S(1)}, u32[]{:S(2)}, u32[]{:S(2)}) async-start(f32[4,1,31680]{2,1,0:T(1,128)} %reshape.27), calls=%async_computation | async-start | bytes 1015808 | tf_op jit(solution)/shard_map/all_to_all | solution.py:40
Sparse Core Ops, SparseCore 0:
  10.2 74.4 all-gather.2
where the time goes:
time: 128 us
  blocking collectives  53.7 us (42%)
  local copies, waits for them, and re-layouts  28.5 us (22%)
  matrix products  22 us (17%)
  between operations  14.1 us (11%)
  other arithmetic  5.58 us (4%)
  starting transfers between devices  3.76 us (3%)
    psum x1, blocking collectives, shards(): traces = lax.psum(traces_local, 'orb')  19.3 us
    psum x1, blocking collectives, shards(): fock_ov = lax.psum(fock_part, 'vec')  17.7 us
    all_gather x1, blocking collectives, shards(): amplitudes = lax.all_gather(singles, 'orb', axis=0, tiled=True)  16.7 us
    unnamed x7, local copies, waits for them, and re-layouts  14.9 us
    dot_general x1, matrix products, dress_left(): jnp.einsum('qin,ia->qan', occ_all, amp_cols, precision=lax.Precision.HIGH...  14.5 us
    all_to_all x3, local copies, waits for them, and re-layouts, shards(): lax.all_to_all(ov_block, 'vec', split_axis=2, concat_axis=0, tiled=True)  7.57 us
    dot_general x2, matrix products, dress_right(): jnp.einsum('qrj,ja->qra', occ_cols, amplitudes, precision=lax.Precision.H...  6.66 us
    add x1, local copies, waits for them, and re-layouts, dress_right(): matrix_rows[:, :, occ_width:] + extra_term  5.96 us
  transfers between devices with their start and end apart: 2, of which 0 were waited for; matrix products, arithmetic and copies ran while one was open for 24% of the time, Pallas kernels for 0%

commit v1 on v0

--- a/solution.py
+++ b/solution.py
@@ -2,6 +2,18 @@
 import jax.numpy as jnp
 from jax import lax
 from jax.sharding import PartitionSpec as P
+
+
+def sent_to_each(x, axis, split, join):
+    ways, here = (lax.axis_size(axis), lax.axis_index(axis))
+    width = x.shape[split] // ways
+    turned = jnp.roll(x, -here * width, axis=split)
+    got = [lax.slice_in_dim(turned, 0, width, axis=split)]
+    for far in range(1, ways):
+        sent = lax.slice_in_dim(turned, far * width, (far + 1) * width, axis=split)
+        got.append(lax.ppermute(sent, axis, [(d, (d + far) % ways) for d in range(ways)]))
+    line = jnp.concatenate(got[::-1], axis=join)
+    return jnp.roll(line, (here + 1) * got[0].shape[join], axis=join)
 
 
 def dress_right(matrix_rows, amplitudes):
@@ -37,7 +49,7 @@
         jnp.einsum("q,qia->ia", traces, ov_block, precision=lax.Precision.HIGHEST) / total_vectors
     )
     fock_ov = lax.psum(fock_part, "vec")
-    pair_blocks = lax.all_to_all(ov_block, "vec", split_axis=2, concat_axis=0, tiled=True)
+    pair_blocks = sent_to_each(ov_block, "vec", 2, 0)
     return (dressed_vir, pair_blocks, fock_ov)
 
 

time: 128 us -> 114 us (0.89)
  local copies, waits for them, and re-layouts: 28.5 us -> 4.7 us
  waiting for transfers between devices: 0.02 us -> 14 us
  other arithmetic: 5.58 us -> 3.92 us
  matrix products: 22 us -> 20.6 us
    all_gather x1, waiting for transfers between devices: 0.01 us -> 13.9 us  [shards(): occ_all = lax.all_gather(chol_occ, 'orb', axis=1, tiled=True)]
    unnamed x7 -> x15, local copies, waits for them, and re-layouts: 14.9 us -> 3.61 us
    all_to_all x3 -> x0, local copies, waits for them, and re-layouts: 7.57 us -> none  [shards(): lax.all_to_all(ov_block, 'vec', split_axis=2, concat_axis=0, tiled=True)]
    add x1 -> x0, local copies, waits for them, and re-layouts: 5.96 us -> none  [dress_right(): matrix_rows[:, :, occ_width:] + extra_term]
    all_to_all x1 -> x0, starting transfers between devices: 3.72 us -> none  [shards(): lax.all_to_all(ov_block, 'vec', split_axis=2, concat_axis=0, tiled=True)]
    ppermute x0 -> x3, starting transfers between devices: none -> 3.49 us  [sent_to_each(): lax.ppermute(sent, axis, [(d, (d + far) % ways) for d in range(ways)])]
    all_to_all x1 -> x0, other arithmetic: 2.12 us -> none  [shards(): lax.all_to_all(ov_block, 'vec', split_axis=2, concat_axis=0, tiled=True)]
  transfers between devices with their start and end apart: 2 -> 4, of which waited for: 0 -> 1; matrix products, arithmetic and copies ran while one was open for 24% -> 4% of each run, Pallas kernels for 0% -> 0%
where the time goes in v1:
time: 114 us
  blocking collectives  52.9 us (46%)
  matrix products  20.6 us (18%)
  between operations  14.3 us (13%)
  waiting for transfers between devices  14 us (12%)
  local copies, waits for them, and re-layouts  4.7 us (4%)
  other arithmetic  3.92 us (3%)
  starting transfers between devices  3.53 us (3%)
    psum x1, blocking collectives, shards(): traces = lax.psum(traces_local, 'orb')  18.6 us
    psum x1, blocking collectives, shards(): fock_ov = lax.psum(fock_part, 'vec')  17.5 us
    all_gather x1, blocking collectives, shards(): amplitudes = lax.all_gather(singles, 'orb', axis=0, tiled=True)  16.7 us
    dot_general x1, matrix products, dress_left(): jnp.einsum('qin,ia->qan', occ_all, amp_cols, precision=lax.Precision.HIGH...  14.3 us
    all_gather x1, waiting for transfers between devices, shards(): occ_all = lax.all_gather(chol_occ, 'orb', axis=1, tiled=True)  13.9 us
    dot_general x2, matrix products, dress_right(): jnp.einsum('qrj,ja->qra', occ_cols, amplitudes, precision=lax.Precision.H...  5.46 us
    unnamed x15, local copies, waits for them, and re-layouts  3.61 us
    ppermute x3, starting transfers between devices, sent_to_each(): lax.ppermute(sent, axis, [(d, (d + far) % ways) for d in range(ways)])  3.49 us
  transfers between devices with their start and end apart: 4, of which 1 were waited for; matrix products, arithmetic and copies ran while one was open for 4% of the time, Pallas kernels for 0%

profile of v1, /device:TPU:0, one launch (start us, length us, event | category | flops | bytes accessed | tf_op | source)
XLA Modules:
  0.0 113.8 jit_solution(10011405049514472887)
XLA Ops:
  7.2 0.0 copy-start.1
  7.2 0.0 all-gather.3.cloned.1.call-start
  7.2 2.3 %copy.10 = f32[11,12,1056]{2,0,1:T(8,128)} copy(f32[11,12,1056]{2,1,0:T(8,128)} %param.3) | data formatting | bytes 1115136 | tf_op args[0]
  9.5 0.0 copy-start
  9.5 0.0 all-gather.3.cloned.1.call-update
  9.5 0.0 copy-done.1
  9.6 16.7 %all-gather = f32[8,12,960]{2,1,0:T(8,128)S(1)} all-gather(f32[1,12,960]{2,1,0:T(8,128)S(1)} %bitcast.13), channel_id=1, replica_groups=mesh['vec'=4,'orb'=8] {'orb'}, dimensions={0}, use_global_device_ids=true | all-gather | bytes 414720 | tf_op jit(solution)/shard_map/all_gather | solution.py:31
  26.4 0.0 copy-done
  26.4 0.7 convolution_add_fusion
  27.1 0.5 fusion.3
  27.6 1.0 fusion.11
  28.6 2.4 %collective-permute-start = (f32[11,12,240]{2,1,0:T(8,128)}, f32[11,12,240]{2,1,0:T(8,128)S(1)}, u32[]{:S(2)}, u32[]{:S(2)}) collective-permute-start(f32[11,12,240]{2,1,0:T(8,128)} %get-tuple-element.14), channel_id=1, source_target_pairs={{0,24},{8,0},{16,8},{24,16},{1,25},{9,1},{17,9},{25,17},{2,26},{10... | collective-permute-start | bytes 380168 | tf_op jit(solution)/shard_map/ppermute | solution.py:14
  30.9 0.6 collective-permute-start.1
  31.5 0.1 fusion.5
  31.6 0.2 multiply_reduce_fusion
  31.8 0.5 collective-permute-start.2
  32.3 18.6 %psum.14 = f32[11]{0:T(128)S(1)} all-reduce(f32[11]{0:T(128)S(1)} %multiply_reduce_fusion), channel_id=1, replica_groups=mesh['vec'=4,'orb'=8] {'orb'}, use_global_device_ids=true, to_apply=%region_1.2 | all-reduce | flops 11 | bytes 88 | tf_op jit(solution)/shard_map/psum | solution.py:45
  51.0 0.8 fusion.1
  51.8 17.5 %psum.15 = f32[12,960]{1,0:T(8,128)} all-reduce(f32[12,960]{1,0:T(8,128)S(1)} %bitcast_multiply_fusion), channel_id=1, replica_groups=mesh['vec'=4,'orb'=8] {'vec'}, use_global_device_ids=true, to_apply=%region_2.3 | all-reduce | flops 11520 | bytes 92160 | tf_op jit(solution)/shard_map/psum | solution.py:51
  69.4 0.0 collective-permute-done
  69.4 0.0 collective-permute-done.1
  69.4 0.0 collective-permute-done.2
  69.6 0.1 constant_dynamic-slice_fusion
  69.6 1.1 copy.13
  70.8 13.9 %all-gather.3.cloned.1.call-done = f32[11,96,1056]{2,0,1:T(8,128)} async-done(((f32[11,12,1056]{2,0,1:T(8,128)}), f32[11,96,1056]{2,0,1:T(8,128)}) %all-gather.3.cloned.1.call-update) | async-done | bytes 4460560 | tf_op jit(solution)/shard_map/all_gather | solution.py:36
  84.7 14.3 %bitcast_subtract_fusion = f32[11,120,1056]{1,2,0:T(8,128)S(1)} fusion(f32[11,120,1056]{1,2,0:T(8,128)} %param.4, f32[11,96,1056]{2,0,1:T(8,128)} %all-gather.3.cloned.1.call-done, f32[96,960]{1,0:T(8,128)S(1)} %reshape.21, s32[]{:T(128)S(6)} %select_n.34), kind=kOutput, calls=%fused_computation.1 | convolution fusion | flops 1607189760 | bytes 15661060 | tf_op jit(solution)/shard_map/qin,ia->qan/dot_general | solution.py:27
  99.0 4.7 %slice_add_fusion = f32[11,120,960]{1,2,0:T(8,128)S(1)} fusion(f32[11,120,1056]{1,2,0:T(8,128)S(1)} %bitcast_subtract_fusion, f32[96,960,1]{1,0,2:T(8,128)S(1)} %reshape.23), kind=kOutput, calls=%fused_computation.2 | convolution fusion | flops 1461081600 | bytes 11013120 | tf_op jit(solution)/shard_map/qrj,ja->qra/dot_general | solution.py:22
  103.8 3.2 %pad_maximum_fusion = f32[11,120,1056]{1,2,0:T(8,128)} fusion(f32[11,120,960]{1,2,0:T(8,128)S(1)} %slice_add_fusion, f32[11,120,96]{1,2,0:T(8,128)S(1)} %slice.32), kind=kLoop, calls=%fused_computation | loop fusion | flops 1393920 | bytes 11151360 | tf_op jit(solution)/shard_map/concatenate | solution.py:23
  (13 shorter events, 0.3 us)
Async XLA Ops:
  7.2 2.4 %copy-start.1 = (f32[12,960]{1,0:T(8,128)S(1)}, f32[12,960]{1,0:T(8,128)}, u32[]{:S(2)}) copy-start(f32[12,960]{1,0:T(8,128)} %param.5) | copy-start | bytes 138244
  7.2 77.5 %all-gather.3.cloned.1.call-start = ((), (), s32[]{:S(2)}) async-start(), calls=%async_computation | async-start | bytes 7962624 | tf_op jit(solution)/shard_map/all_gather | solution.py:36
  9.5 16.9 %copy-start = (f32[11,12,1056]{2,1,0:T(8,128)S(1)}, f32[11,12,1056]{2,1,0:T(8,128)}, u32[]{:S(2)}) copy-start(f32[11,12,1056]{2,1,0:T(8,128)} %param.3) | copy-start | bytes 1672708
  28.6 40.8 %collective-permute-start = (f32[11,12,240]{2,1,0:T(8,128)}, f32[11,12,240]{2,1,0:T(8,128)S(1)}, u32[]{:S(2)}, u32[]{:S(2)}) collective-permute-start(f32[11,12,240]{2,1,0:T(8,128)} %get-tuple-element.14), channel_id=1, source_target_pairs={{0,24},{8,0},{16,8},{24,16},{1,25},{9,1},{17,9},{25,17},{2,26},{10... | collective-permute-start | bytes 380168 | tf_op jit(solution)/shard_map/ppermute | solution.py:14
  30.9 38.5 %collective-permute-start.1 = (f32[11,12,240]{2,1,0:T(8,128)}, f32[11,12,240]{2,1,0:T(8,128)S(1)}, u32[]{:S(2)}, u32[]{:S(2)}) collective-permute-start(f32[11,12,240]{2,1,0:T(8,128)} %get-tuple-element.13), channel_id=1, source_target_pairs={{0,16},{8,24},{16,0},{24,8},{1,17},{9,25},{17,1},{25,9},{2,18},{10... | collective-permute-start | bytes 380168 | tf_op jit(solution)/shard_map/ppermute | solution.py:14
  31.8 37.7 %collective-permute-start.2 = (f32[11,12,240]{2,1,0:T(8,128)}, f32[11,12,240]{2,1,0:T(8,128)S(1)}, u32[]{:S(2)}, u32[]{:S(2)}) collective-permute-start(f32[11,12,240]{2,1,0:T(8,128)} %get-tuple-element.12), channel_id=1, source_target_pairs={{0,8},{8,16},{16,24},{24,0},{1,9},{9,17},{17,25},{25,1},{2,10},{10... | collective-permute-start | bytes 380168 | tf_op jit(solution)/shard_map/ppermute | solution.py:14
Sparse Core Ops, SparseCore 0:
  10.2 74.4 all-gather.2
